TPU v7x, 256 devices: a whole 4x4x8 slice. The times are simulated.
256 devices in a mesh: sec: 2 (over core), var: 32 (over y, z), trait: 4 (over x).
Axes of the slice: x: 4, y: 4, z: 8, core: 2. Of those that a mesh axis runs over, the one named last changes fastest.
Arguments:
- z_typed: bfloat16 [262144, 512], P(('sec', 'var'), 'trait'), may hold values from -6 to 6
- band_inverse: bfloat16 [2048, 128, 384], P(('sec', 'var')), may hold values from -0.3125 to 0.3125
- ld_untyped: bfloat16 [4096, 128, 512], P(('sec', 'var')), may hold values from -0.375 to 0.375
- trait_mix: bfloat16 [512, 512], replicated, may hold values from -0.25 to 0.25
- win_start: int32 [4096], P(('sec', 'var')), may hold values from 0 to 2047, as said below
- win_count: int32 [4096], P(('sec', 'var')), may hold values from 1 to 4, as said below
Outputs:
- imputed_mixed: bfloat16 [524288, 512], P(('sec', 'var'), 'trait')
Inputs may be any that keep to these rules, and one draw needn't show every extreme that they name: Windows follow chromosome order: within the 64 untyped blocks of one index g of sec+var, win_start never falls, and every window lies in typed blocks g * 32 - 32 to (g + 1) * 32 + 31; the first window of each index starts at its lower end (or at 0) and the last one ends at its upper end (or at the chromosome's end). win_start + win_count never exceeds 2048.
All inputs are finite; a program needn't handle non-finite values.
Results may differ from a plain program's by a relative error of at most 0.0057.
Values may be sent and summed in bfloat16 or wider, within the bound.
No kernel may reach another device: no remote copies, remote signals or barrier semaphores. Data moves between devices by JAX's collectives and lax.ppermute only.
A program may use at most 64 MiB of HBM per device.

v0:
```python
import jax
import jax.numpy as jnp
from jax import lax
from jax.sharding import PartitionSpec as P

BLK = 128
WIN = 4


def padded_2(cells, sides, width):
    for axis, dim in sides:
        count = lax.axis_size(axis)
        ends = count - 1
        head = lax.slice_in_dim(cells, 0, width, axis=dim)
        tail = lax.slice_in_dim(cells, cells.shape[dim] - width, cells.shape[dim], axis=dim)
        cells = jnp.concatenate(
            [
                lax.ppermute(tail, axis, [(i, (i + 1) % count) for i in range(ends)]),
                cells,
                lax.ppermute(head, axis, [((i + 1) % count, i) for i in range(ends)]),
            ],
            axis=dim,
        )
    return cells


def on_device(z_typed, band_inverse, ld_untyped, trait_mix, win_start, win_count):
    trait_cols = z_typed.shape[1]
    typed_blocks = z_typed.shape[0] // BLK
    padded = padded_2(z_typed, ((("sec", "var"), 0),), BLK)
    stacked = jnp.concatenate(
        [
            padded[k * BLK : (k + typed_blocks) * BLK].reshape(typed_blocks, BLK, trait_cols)
            for k in range(3)
        ],
        axis=1,
    )
    whitened = jnp.einsum(
        "bij,bjc->bic", band_inverse, stacked, preferred_element_type=jnp.float32
    ).astype(jnp.bfloat16)
    whitened_rows = whitened.reshape(typed_blocks * BLK, trait_cols)
    column_start = lax.axis_index("trait") * trait_cols
    mix_cols = lax.dynamic_slice_in_dim(trait_mix, column_start, trait_cols, 1)
    mixed_sums = jnp.dot(
        lax.all_gather(whitened_rows, "trait", axis=1, tiled=True),
        mix_cols,
        preferred_element_type=jnp.float32,
    )
    mixed = mixed_sums.astype(jnp.bfloat16).reshape(typed_blocks, BLK, trait_cols)
    window_steps = jnp.arange(WIN, dtype=jnp.int32)
    usable = window_steps[None, :] < win_count[:, None]
    untyped_blocks = win_start.shape[0]
    extended = padded_2(mixed, ((("sec", "var"), 0),), typed_blocks)
    local_first = win_start - lax.axis_index(("sec", "var")) * typed_blocks + typed_blocks
    wanted = jnp.clip(local_first[:, None] + window_steps[None, :], 0, 3 * typed_blocks - 1)
    picked = extended[wanted]
    chosen = jnp.where(usable[:, :, None, None], picked, jnp.zeros_like(picked))
    window_rows = chosen.reshape(untyped_blocks, WIN * BLK, trait_cols)
    imputed = jnp.einsum(
        "uij,ujc->uic", ld_untyped, window_rows, preferred_element_type=jnp.float32
    ).astype(jnp.bfloat16)
    return imputed.reshape(untyped_blocks * BLK, trait_cols)


def solution(mesh):
    in_specs = (
        P(("sec", "var"), "trait"),
        P(("sec", "var"), None, None),
        P(("sec", "var"), None, None),
        P(),
        P(("sec", "var")),
        P(("sec", "var")),
    )
    out_specs = P(("sec", "var"), "trait")
    return jax.shard_map(
        on_device, mesh=mesh, in_specs=in_specs, out_specs=out_specs, check_vma=False
    )
```

profile of v0, /device:TPU:24, one launch (start us, length us, event | category | flops | bytes accessed | tf_op | source)
XLA Modules:
  0.0 152.1 jit_solution(10747132638285355354)
XLA Ops:
  6.5 0.0 copy-start
  6.5 0.0 all-gather.2.cloned.1.call-start
  6.5 0.9 fusion.12
  7.5 3.9 %collective-permute-start = (bf16[128,128]{1,0:T(8,128)(2,1)S(1)}, bf16[128,128]{1,0:T(8,128)(2,1)S(1)}, u32[]{:S(2)}, u32[]{:S(2)}) collective-permute-start(bf16[128,128]{1,0:T(8,128)(2,1)S(1)} %get-tuple-element.7), channel_id=1, source_target_pairs={{0,4},{4,8},{8,12},{12,16},{16,20},{20,24},{24,28},{28,32},{32,36}... | collective-permute-start | bytes 98312 | tf_op jit(solution)/shard_map/ppermute | solution.py:18
  11.4 6.0 %collective-permute-start.1 = (bf16[128,128]{1,0:T(8,128)(2,1)S(1)}, bf16[128,128]{1,0:T(8,128)(2,1)S(1)}, u32[]{:S(2)}, u32[]{:S(2)}) collective-permute-start(bf16[128,128]{1,0:T(8,128)(2,1)S(1)} %get-tuple-element.8), channel_id=1, source_target_pairs={{4,0},{8,4},{12,8},{16,12},{20,16},{24,20},{28,24},{32,28},{36,32}... | collective-permute-start | bytes 98312 | tf_op jit(solution)/shard_map/ppermute | solution.py:20
  17.5 0.0 collective-permute-done
  17.5 1.6 %collective-permute-done.1 = bf16[128,128]{1,0:T(8,128)(2,1)S(1)} collective-permute-done((bf16[128,128]{1,0:T(8,128)(2,1)S(1)}, bf16[128,128]{1,0:T(8,128)(2,1)S(1)}, u32[]{:S(2)}, u32[]{:S(2)}) %collective-permute-start.1) | collective-permute-done | bytes 32800 | tf_op jit(solution)/shard_map/ppermute | solution.py:20
  19.0 1.7 %pad_maximum_fusion.2 = (bf16[4096,128]{1,0:T(8,128)(2,1)S(1)}, bf16[4096,128]{1,0:T(8,128)(2,1)S(1)}) fusion(bf16[4096,128]{1,0:T(8,128)(2,1)} %param.6, bf16[128,128]{1,0:T(8,128)(2,1)S(1)} %collective-permute-done, bf16[128,128]{1,0:T(8,128)(2,1)S(1)} %collective-permute-done.1), kind=kLoop, calls=%fused_computation.13 | loop fusion | flops 4194304 | bytes 3211264 | tf_op jit(solution)/shard_map/concatenate | solution.py:16
  20.7 0.0 copy-done
  20.8 3.2 %fusion.6 = bf16[32,128,128]{1,2,0:T(8,128)(2,1)} fusion(bf16[32,128,384]{2,1,0:T(8,128)(2,1)S(1)} %copy-done, bf16[32,128,128]{2,1,0:T(8,128)(2,1)S(1)} %bitcast.26, bf16[32,128,128]{2,1,0:T(8,128)(2,1)} %bitcast.24, bf16[32,128,128]{2,1,0:T(8,128)(2,1)S(1)} %bitcast.25), kind=kOutput, calls=%fused_computation.11 | convolution fusion | flops 412614656 | bytes 7340032 | tf_op jit(solution)/shard_map/bij,bjc->bic/dot_general | solution.py:38
  24.0 0.0 copy-start.1
  24.0 0.0 copy-start.2
  24.0 0.0 all-gather.2.cloned.1.call-update
  24.0 55.4 %all-gather.2.cloned.1.call-done = bf16[4096,512]{1,0:T(8,128)(2,1)} async-done(((bf16[4096,128]{1,0:T(8,128)(2,1)}), bf16[4096,512]{1,0:T(8,128)(2,1)}) %all-gather.2.cloned.1.call-update) | async-done | bytes 4194320 | tf_op jit(solution)/shard_map/all_gather | solution.py:45
  79.4 4.4 %convolution_convert_fusion = bf16[4096,128]{1,0:T(8,128)(2,1)} fusion(bf16[4096,512]{1,0:T(8,128)(2,1)} %all-gather.2.cloned.1.call-done, bf16[512,512]{1,0:T(8,128)(2,1)} %param.9, s32[]{:T(128)S(6)} %select_n.18), kind=kOutput, calls=%fused_computation.2 | convolution fusion | flops 537395200 | bytes 5373956 | tf_op jit(solution)/shard_map/dot_general | solution.py:44
  83.8 5.5 %collective-permute-start.3 = (bf16[32,128,128]{2,1,0:T(8,128)(2,1)}, bf16[32,128,128]{2,1,0:T(8,128)(2,1)}, u32[]{:S(2)}, u32[]{:S(2)}) collective-permute-start(bf16[32,128,128]{2,1,0:T(8,128)(2,1)} %bitcast.5), channel_id=1, source_target_pairs={{4,0},{8,4},{12,8},{16,12},{20,16},{24,20},{28,24},{32,28},{36,32}... | collective-permute-start | bytes 3145736 | tf_op jit(solution)/shard_map/ppermute | solution.py:20
  89.3 1.9 %collective-permute-start.2 = (bf16[32,128,128]{2,1,0:T(8,128)(2,1)}, bf16[32,128,128]{2,1,0:T(8,128)(2,1)}, u32[]{:S(2)}, u32[]{:S(2)}) collective-permute-start(bf16[32,128,128]{2,1,0:T(8,128)(2,1)} %bitcast.5), channel_id=1, source_target_pairs={{0,4},{4,8},{8,12},{12,16},{16,20},{20,24},{24,28},{28,32},{32,36}... | collective-permute-start | bytes 3145736 | tf_op jit(solution)/shard_map/ppermute | solution.py:18
  91.3 0.0 copy-done.1
  91.3 0.1 iota_compare_fusion
  91.4 0.1 broadcast_in_dim.21
  91.5 0.0 copy-done.2
  91.5 0.1 compare_select_fusion
  91.6 0.1 reshape.93
  91.8 19.4 %collective-permute-done.3 = bf16[32,128,128]{2,1,0:T(8,128)(2,1)} collective-permute-done((bf16[32,128,128]{2,1,0:T(8,128)(2,1)}, bf16[32,128,128]{2,1,0:T(8,128)(2,1)}, u32[]{:S(2)}, u32[]{:S(2)}) %collective-permute-start.3) | collective-permute-done | bytes 1048608 | tf_op jit(solution)/shard_map/ppermute | solution.py:20
  111.2 6.2 %collective-permute-done.2 = bf16[32,128,128]{2,1,0:T(8,128)(2,1)} collective-permute-done((bf16[32,128,128]{2,1,0:T(8,128)(2,1)}, bf16[32,128,128]{2,1,0:T(8,128)(2,1)}, u32[]{:S(2)}, u32[]{:S(2)}) %collective-permute-start.2) | collective-permute-done | bytes 1048608 | tf_op jit(solution)/shard_map/ppermute | solution.py:18
  117.4 3.3 %pad_maximum_fusion = bf16[96,128,128]{2,1,0:T(8,128)(2,1)} fusion(bf16[32,128,128]{2,1,0:T(8,128)(2,1)} %collective-permute-done.3, bf16[32,128,128]{2,1,0:T(8,128)(2,1)} %bitcast.5, bf16[32,128,128]{2,1,0:T(8,128)(2,1)} %collective-permute-done.2), kind=kLoop, calls=%fused_computation.9 | loop fusion | flops 3145728 | bytes 6291456 | tf_op jit(solution)/shard_map/concatenate | solution.py:16
  120.7 10.5 %gather_fusion = bf16[256,128,128]{2,1,0:T(8,128)(2,1)} fusion(bf16[96,128,128]{2,1,0:T(8,128)(2,1)} %pad_maximum_fusion, s32[1024]{0:T(1024)S(1)} %pad_clamp_fusion), kind=kCustom, calls=%fused_computation | custom fusion | bytes 16778240 | tf_op jit(solution)/shard_map/gather | solution.py:56
  131.2 7.0 %bitcast_select_fusion = bf16[64,512,128]{2,1,0:T(8,128)(2,1)S(1)} fusion(pred[64,512]{1,0:T(8,128)(4,1)S(1)} %bitcast.28, bf16[64,512,128]{2,1,0:T(8,128)(2,1)} %bitcast.23), kind=kLoop, calls=%fused_computation.1 | loop fusion | flops 4194304 | bytes 16809984 | tf_op jit(solution)/shard_map/jit(_where)/select_n | solution.py:57
  138.2 7.0 %convolution_convert_fusion.1 = bf16[64,128,128]{1,2,0:T(8,128)(2,1)} fusion(bf16[64,128,512]{2,1,0:T(8,128)(2,1)} %param.8, bf16[64,512,128]{2,1,0:T(8,128)(2,1)S(1)} %bitcast_select_fusion), kind=kOutput, calls=%fused_computation.10 | convolution fusion | flops 1074790400 | bytes 18874368 | tf_op jit(solution)/shard_map/uij,ujc->uic/dot_general | solution.py:59
  (3 shorter events, 0.0 us)
Async XLA Ops:
  6.5 14.2 %copy-start = (bf16[32,128,384]{2,1,0:T(8,128)(2,1)S(1)}, bf16[32,128,384]{2,1,0:T(8,128)(2,1)}, u32[]{:S(2)}) copy-start(bf16[32,128,384]{2,1,0:T(8,128)(2,1)} %param.7) | copy-start | bytes 9437188
  6.5 72.9 %all-gather.2.cloned.1.call-start = ((), (), s32[]{:S(2)}) async-start(), calls=%async_computation | async-start | bytes 5242880 | tf_op jit(solution)/shard_map/all_gather | solution.py:45
  7.5 10.0 %collective-permute-start = (bf16[128,128]{1,0:T(8,128)(2,1)S(1)}, bf16[128,128]{1,0:T(8,128)(2,1)S(1)}, u32[]{:S(2)}, u32[]{:S(2)}) collective-permute-start(bf16[128,128]{1,0:T(8,128)(2,1)S(1)} %get-tuple-element.7), channel_id=1, source_target_pairs={{0,4},{4,8},{8,12},{12,16},{16,20},{20,24},{24,28},{28,32},{32,36}... | collective-permute-start | bytes 98312 | tf_op jit(solution)/shard_map/ppermute | solution.py:18
  11.4 7.6 %collective-permute-start.1 = (bf16[128,128]{1,0:T(8,128)(2,1)S(1)}, bf16[128,128]{1,0:T(8,128)(2,1)S(1)}, u32[]{:S(2)}, u32[]{:S(2)}) collective-permute-start(bf16[128,128]{1,0:T(8,128)(2,1)S(1)} %get-tuple-element.8), channel_id=1, source_target_pairs={{4,0},{8,4},{12,8},{16,12},{20,16},{24,20},{28,24},{32,28},{36,32}... | collective-permute-start | bytes 98312 | tf_op jit(solution)/shard_map/ppermute | solution.py:20
  24.0 67.3 %copy-start.1 = (s32[64]{0:T(128)S(1)}, s32[64]{0:T(128)}, u32[]{:S(2)}) copy-start(s32[64]{0:T(128)} %param.11) | copy-start | bytes 772
  24.0 67.5 %copy-start.2 = (s32[64]{0:T(128)S(1)}, s32[64]{0:T(128)}, u32[]{:S(2)}) copy-start(s32[64]{0:T(128)} %param.10) | copy-start | bytes 772
  83.8 27.3 %collective-permute-start.3 = (bf16[32,128,128]{2,1,0:T(8,128)(2,1)}, bf16[32,128,128]{2,1,0:T(8,128)(2,1)}, u32[]{:S(2)}, u32[]{:S(2)}) collective-permute-start(bf16[32,128,128]{2,1,0:T(8,128)(2,1)} %bitcast.5), channel_id=1, source_target_pairs={{4,0},{8,4},{12,8},{16,12},{20,16},{24,20},{28,24},{32,28},{36,32}... | collective-permute-start | bytes 3145736 | tf_op jit(solution)/shard_map/ppermute | solution.py:20
  89.3 28.1 %collective-permute-start.2 = (bf16[32,128,128]{2,1,0:T(8,128)(2,1)}, bf16[32,128,128]{2,1,0:T(8,128)(2,1)}, u32[]{:S(2)}, u32[]{:S(2)}) collective-permute-start(bf16[32,128,128]{2,1,0:T(8,128)(2,1)} %bitcast.5), channel_id=1, source_target_pairs={{0,4},{4,8},{8,12},{12,16},{16,20},{20,24},{24,28},{28,32},{32,36}... | collective-permute-start | bytes 3145736 | tf_op jit(solution)/shard_map/ppermute | solution.py:18
Sparse Core Ops, SparseCore 0:
  24.1 55.2 all-gather.1
where the time goes:
time: 152 us
  waiting for transfers between devices  82.6 us (54%)
  starting transfers between devices  17.4 us (11%)
  matrix products  14.7 us (10%)
  between operations  13.5 us (9%)
  other arithmetic  12.2 us (8%)
  local copies, waits for them, and re-layouts  11.7 us (8%)
    all_gather x1, waiting for transfers between devices, on_device(): lax.all_gather(whitened_rows, 'trait', axis=1, tiled=True)  55.4 us
    ppermute x2, waiting for transfers between devices, padded_2(): lax.ppermute(head, axis, [((i + 1) % count, i) for i in range(ends)])  21 us
    ppermute x2, starting transfers between devices, padded_2(): lax.ppermute(head, axis, [((i + 1) % count, i) for i in range(ends)])  11.5 us
    gather x1, local copies, waits for them, and re-layouts, on_device(): picked = extended[wanted]  10.5 us
    dot_general x1, matrix products, on_device(): jnp.einsum('uij,ujc->uic', ld_untyped, window_rows, preferred_element_typ...  7.04 us
    select_n x1, other arithmetic, on_device(): chosen = jnp.where(usable[:, :, None, None], picked, jnp.zeros_like(picked))  7.01 us
    ppermute x2, waiting for transfers between devices, padded_2(): lax.ppermute(tail, axis, [(i, (i + 1) % count) for i in range(ends)])  6.23 us
    ppermute x2, starting transfers between devices, padded_2(): lax.ppermute(tail, axis, [(i, (i + 1) % count) for i in range(ends)])  5.87 us
  transfers between devices with their start and end apart: 5, of which 4 were waited for; matrix products, arithmetic and copies ran while one was open for 0% of the time, Pallas kernels for 0%

commit v1 on v0

--- a/solution.py
+++ b/solution.py
@@ -2,9 +2,33 @@
 import jax.numpy as jnp
 from jax import lax
 from jax.sharding import PartitionSpec as P
+from jax.lax import axis_index, axis_size, ppermute
 
 BLK = 128
 WIN = 4
+
+
+def _remake_leaf(vector, mesh_ax, dim_i):
+    passed, val, z1 = (axis_size(mesh_ax), axis_index(mesh_ax), vector.shape[dim_i])
+    table = tuple(((t, (t + 1) % passed) for t in range(passed)))
+    store = tuple(((t, (t - 1) % passed) for t in range(passed)))
+    r_now = jnp.zeros(
+        (*vector.shape[:dim_i], passed * z1, *vector.shape[dim_i + 1 :]), vector.dtype
+    )
+    r_now = lax.dynamic_update_slice_in_dim(r_now, vector, val * z1, axis=dim_i)
+    later = near = vector
+    tall = passed // 2
+    q = 1
+    while q < tall + 1:
+        later = ppermute(later, axis_name=mesh_ax, perm=table)
+        r_now = lax.dynamic_update_slice_in_dim(r_now, later, (val - q) % passed * z1, axis=dim_i)
+        if q < passed - tall:
+            near = ppermute(near, axis_name=mesh_ax, perm=store)
+            r_now = lax.dynamic_update_slice_in_dim(
+                r_now, near, (val + q) % passed * z1, axis=dim_i
+            )
+        q += 1
+    return r_now
 
 
 def padded_2(cells, sides, width):
@@ -42,9 +66,7 @@
     column_start = lax.axis_index("trait") * trait_cols
     mix_cols = lax.dynamic_slice_in_dim(trait_mix, column_start, trait_cols, 1)
     mixed_sums = jnp.dot(
-        lax.all_gather(whitened_rows, "trait", axis=1, tiled=True),
-        mix_cols,
-        preferred_element_type=jnp.float32,
+        _remake_leaf(whitened_rows, "trait", 1), mix_cols, preferred_element_type=jnp.float32
     )
     mixed = mixed_sums.astype(jnp.bfloat16).reshape(typed_blocks, BLK, trait_cols)
     window_steps = jnp.arange(WIN, dtype=jnp.int32)

time: 152 us -> 131 us (0.86)
  waiting for transfers between devices: 82.6 us -> 66.8 us
  between operations: 13.5 us -> 0.17 us
  local copies, waits for them, and re-layouts: 11.7 us -> 16.7 us
  starting transfers between devices: 17.4 us -> 21.3 us
    all_gather x1 -> x0, waiting for transfers between devices: 55.4 us -> none  [on_device(): lax.all_gather(whitened_rows, 'trait', axis=1, tiled=True)]
    ppermute x0 -> x3, waiting for transfers between devices: none -> 41.9 us  [the longest x2 41.9 us: _remake_leaf(): later = ppermute(later, axis_name=mesh_ax, perm=table)]
    dynamic_update_slice x0 -> x4, local copies, waits for them, and re-layouts: none -> 4.69 us  [the longest x2 1.73 us: _remake_leaf(): lax.dynamic_update_slice_in_dim(r_now, later, (val - q) % passed * z1, ax...]
    ppermute x0 -> x3, starting transfers between devices: none -> 3.51 us  [the longest x2 1.77 us: _remake_leaf(): later = ppermute(later, axis_name=mesh_ax, perm=table)]
    ppermute x2, waiting for transfers between devices: 21 us -> 18.7 us  [padded_2(): lax.ppermute(head, axis, [((i + 1) % count, i) for i in range(ends)])]
  transfers between devices with their start and end apart: 5 -> 7, of which waited for: 4 -> 5; matrix products, arithmetic and copies ran while one was open for 0% -> 4% of each run, Pallas kernels for 0% -> 0%
where the time goes in v1:
time: 131 us; the launch traced here: 130 us
  waiting for transfers between devices  66.8 us (51%)
  starting transfers between devices  21.3 us (16%)
  local copies, waits for them, and re-layouts  16.7 us (13%)
  matrix products  13.4 us (10%)
  other arithmetic  12.2 us (9%)
    ppermute x2, waiting for transfers between devices, _remake_leaf(): later = ppermute(later, axis_name=mesh_ax, perm=table)  41.9 us
    ppermute x2, waiting for transfers between devices, padded_2(): lax.ppermute(head, axis, [((i + 1) % count, i) for i in range(ends)])  18.7 us
    ppermute x2, starting transfers between devices, padded_2(): lax.ppermute(head, axis, [((i + 1) % count, i) for i in range(ends)])  11.8 us
    gather x1, local copies, waits for them, and re-layouts, on_device(): picked = extended[wanted]  10.5 us
    dot_general x1, matrix products, on_device(): jnp.einsum('uij,ujc->uic', ld_untyped, window_rows, preferred_element_typ...  7.04 us
    select_n x1, other arithmetic, on_device(): chosen = jnp.where(usable[:, :, None, None], picked, jnp.zeros_like(picked))  7.01 us
    ppermute x2, waiting for transfers between devices, padded_2(): lax.ppermute(tail, axis, [(i, (i + 1) % count) for i in range(ends)])  6.23 us
    ppermute x2, starting transfers between devices, padded_2(): lax.ppermute(tail, axis, [(i, (i + 1) % count) for i in range(ends)])  6.05 us
  transfers between devices with their start and end apart: 7, of which 5 were waited for; matrix products, arithmetic and copies ran while one was open for 4% of the time, Pallas kernels for 0%

profile of v1, /device:TPU:24, one launch (start us, length us, event | category | flops | bytes accessed | tf_op | source)
XLA Modules:
  0.0 130.5 jit_solution(10135638704301811702)
XLA Ops:
  0.0 0.0 copy-start
  0.0 0.9 fusion.12
  0.9 3.9 %collective-permute-start = (bf16[128,128]{1,0:T(8,128)(2,1)S(1)}, bf16[128,128]{1,0:T(8,128)(2,1)S(1)}, u32[]{:S(2)}, u32[]{:S(2)}) collective-permute-start(bf16[128,128]{1,0:T(8,128)(2,1)S(1)} %get-tuple-element.7), channel_id=1, source_target_pairs={{0,4},{4,8},{8,12},{12,16},{16,20},{20,24},{24,28},{28,32},{32,36}... | collective-permute-start | bytes 98312 | tf_op jit(solution)/shard_map/ppermute | solution.py:42
  4.9 6.0 %collective-permute-start.1 = (bf16[128,128]{1,0:T(8,128)(2,1)S(1)}, bf16[128,128]{1,0:T(8,128)(2,1)S(1)}, u32[]{:S(2)}, u32[]{:S(2)}) collective-permute-start(bf16[128,128]{1,0:T(8,128)(2,1)S(1)} %get-tuple-element.8), channel_id=1, source_target_pairs={{4,0},{8,4},{12,8},{16,12},{20,16},{24,20},{28,24},{32,28},{36,32}... | collective-permute-start | bytes 98312 | tf_op jit(solution)/shard_map/ppermute | solution.py:44
  10.9 0.0 collective-permute-done
  10.9 1.6 %collective-permute-done.1 = bf16[128,128]{1,0:T(8,128)(2,1)S(1)} collective-permute-done((bf16[128,128]{1,0:T(8,128)(2,1)S(1)}, bf16[128,128]{1,0:T(8,128)(2,1)S(1)}, u32[]{:S(2)}, u32[]{:S(2)}) %collective-permute-start.1) | collective-permute-done | bytes 32800 | tf_op jit(solution)/shard_map/ppermute | solution.py:44
  12.5 1.7 %pad_maximum_fusion.2 = (bf16[4096,128]{1,0:T(8,128)(2,1)S(1)}, bf16[4096,128]{1,0:T(8,128)(2,1)S(1)}) fusion(bf16[4096,128]{1,0:T(8,128)(2,1)} %param.6, bf16[128,128]{1,0:T(8,128)(2,1)S(1)} %collective-permute-done, bf16[128,128]{1,0:T(8,128)(2,1)S(1)} %collective-permute-done.1), kind=kLoop, calls=%fused_computation.13 | loop fusion | flops 4194304 | bytes 3211264 | tf_op jit(solution)/shard_map/concatenate | solution.py:40
  14.2 0.0 copy-done
  14.2 3.2 %fusion.6 = bf16[32,128,128]{1,2,0:T(8,128)(2,1)} fusion(bf16[32,128,384]{2,1,0:T(8,128)(2,1)S(1)} %copy-done, bf16[32,128,128]{2,1,0:T(8,128)(2,1)S(1)} %bitcast.26, bf16[32,128,128]{2,1,0:T(8,128)(2,1)} %bitcast.24, bf16[32,128,128]{2,1,0:T(8,128)(2,1)S(1)} %bitcast.25), kind=kOutput, calls=%fused_computation.11 | convolution fusion | flops 412614656 | bytes 7340032 | tf_op jit(solution)/shard_map/bij,bjc->bic/dot_general | solution.py:62
  17.4 1.5 %collective-permute-start.2 = (bf16[4096,128]{1,0:T(8,128)(2,1)}, bf16[4096,128]{1,0:T(8,128)(2,1)}, u32[]{:S(2)}, u32[]{:S(2)}) collective-permute-start(bf16[4096,128]{1,0:T(8,128)(2,1)} %bitcast.4), channel_id=1, source_target_pairs={{0,1},{1,2},{2,3},{3,0},{4,5},{5,6},{6,7},{7,4},{8,9},{9,10},{10,1... | collective-permute-start | bytes 3145736 | tf_op jit(solution)/shard_map/ppermute | solution.py:23
  18.9 1.7 %collective-permute-start.3 = (bf16[4096,128]{1,0:T(8,128)(2,1)}, bf16[4096,128]{1,0:T(8,128)(2,1)}, u32[]{:S(2)}, u32[]{:S(2)}) collective-permute-start(bf16[4096,128]{1,0:T(8,128)(2,1)} %bitcast.4), channel_id=1, source_target_pairs={{0,3},{1,0},{2,1},{3,2},{4,7},{5,4},{6,5},{7,6},{8,11},{9,8},{10,9... | collective-permute-start | bytes 3145736 | tf_op jit(solution)/shard_map/ppermute | solution.py:26
  20.7 22.3 %collective-permute-done.2 = bf16[4096,128]{1,0:T(8,128)(2,1)} collective-permute-done((bf16[4096,128]{1,0:T(8,128)(2,1)}, bf16[4096,128]{1,0:T(8,128)(2,1)}, u32[]{:S(2)}, u32[]{:S(2)}) %collective-permute-start.2) | collective-permute-done | bytes 1048608 | tf_op jit(solution)/shard_map/ppermute | solution.py:23
  43.0 0.3 collective-permute-start.4
  43.3 0.3 broadcast_in_dim.27
  43.6 1.5 %constant_dynamic-update-slice_fusion.3 = bf16[4096,512]{1,0:T(8,128)(2,1)S(1)} fusion(bf16[4096,512]{1,0:T(8,128)(2,1)S(1)} %broadcast_in_dim.27, bf16[4096,128]{1,0:T(8,128)(2,1)} %bitcast.4, s32[]{:T(128)S(6)} %select_n.43), kind=kLoop, calls=%fused_computation.23 | loop fusion | bytes 2097156 | tf_op jit(solution)/shard_map/dynamic_update_slice | solution.py:18
  45.1 1.5 %constant_dynamic-update-slice_fusion.2 = bf16[4096,512]{1,0:T(8,128)(2,1)S(1)} fusion(bf16[4096,512]{1,0:T(8,128)(2,1)S(1)} %constant_dynamic-update-slice_fusion.3, bf16[4096,128]{1,0:T(8,128)(2,1)} %collective-permute-done.2, s32[]{:T(128)S(6)} %select_n.45), kind=kLoop, calls=%fused_computation.22 | loop fusion | bytes 2097156 | tf_op jit(solution)/shard_map/dynamic_update_slice | solution.py:24
  46.5 0.0 collective-permute-done.3
  46.5 1.5 %constant_dynamic-update-slice_fusion.1 = bf16[4096,512]{1,0:T(8,128)(2,1)S(1)} fusion(bf16[4096,512]{1,0:T(8,128)(2,1)S(1)} %constant_dynamic-update-slice_fusion.2, bf16[4096,128]{1,0:T(8,128)(2,1)} %collective-permute-done.3, s32[]{:T(128)S(6)} %select_n.47), kind=kLoop, calls=%fused_computation.21 | loop fusion | bytes 2097156 | tf_op jit(solution)/shard_map/dynamic_update_slice | solution.py:27
  48.0 0.0 copy-start.1
  48.0 0.0 copy-start.2
  48.1 19.5 %collective-permute-done.4 = bf16[4096,128]{1,0:T(8,128)(2,1)S(1)} collective-permute-done((bf16[4096,128]{1,0:T(8,128)(2,1)}, bf16[4096,128]{1,0:T(8,128)(2,1)S(1)}, u32[]{:S(2)}, u32[]{:S(2)}) %collective-permute-start.4) | collective-permute-done | bytes 1048608 | tf_op jit(solution)/shard_map/ppermute | solution.py:23
  67.6 0.2 constant_dynamic-update-slice_fusion
  67.8 3.1 %convolution_convert_fusion = bf16[4096,128]{1,0:T(8,128)(2,1)} fusion(bf16[4096,512]{1,0:T(8,128)(2,1)S(1)} %constant_dynamic-update-slice_fusion, bf16[512,512]{1,0:T(8,128)(2,1)} %param.9, s32[]{:T(128)S(6)} %select_n.43), kind=kOutput, calls=%fused_computation.2 | convolution fusion | flops 537395200 | bytes 5373956 | tf_op jit(solution)/shard_map/dot_general | solution.py:68
  71.0 5.7 %collective-permute-start.6 = (bf16[32,128,128]{2,1,0:T(8,128)(2,1)}, bf16[32,128,128]{2,1,0:T(8,128)(2,1)}, u32[]{:S(2)}, u32[]{:S(2)}) collective-permute-start(bf16[32,128,128]{2,1,0:T(8,128)(2,1)} %bitcast.6), channel_id=1, source_target_pairs={{4,0},{8,4},{12,8},{16,12},{20,16},{24,20},{28,24},{32,28},{36,32}... | collective-permute-start | bytes 3145736 | tf_op jit(solution)/shard_map/ppermute | solution.py:44
  76.7 2.1 %collective-permute-start.5 = (bf16[32,128,128]{2,1,0:T(8,128)(2,1)}, bf16[32,128,128]{2,1,0:T(8,128)(2,1)}, u32[]{:S(2)}, u32[]{:S(2)}) collective-permute-start(bf16[32,128,128]{2,1,0:T(8,128)(2,1)} %bitcast.6), channel_id=1, source_target_pairs={{0,4},{4,8},{8,12},{12,16},{16,20},{20,24},{24,28},{28,32},{32,36}... | collective-permute-start | bytes 3145736 | tf_op jit(solution)/shard_map/ppermute | solution.py:42
  78.8 0.0 copy-done.1
  78.8 0.1 iota_compare_fusion
  78.9 0.1 broadcast_in_dim.24
  79.1 0.0 copy-done.2
  79.1 0.1 compare_select_fusion
  79.2 0.1 reshape.93
  79.3 17.1 %collective-permute-done.6 = bf16[32,128,128]{2,1,0:T(8,128)(2,1)} collective-permute-done((bf16[32,128,128]{2,1,0:T(8,128)(2,1)}, bf16[32,128,128]{2,1,0:T(8,128)(2,1)}, u32[]{:S(2)}, u32[]{:S(2)}) %collective-permute-start.6) | collective-permute-done | bytes 1048608 | tf_op jit(solution)/shard_map/ppermute | solution.py:44
  96.4 6.2 %collective-permute-done.5 = bf16[32,128,128]{2,1,0:T(8,128)(2,1)} collective-permute-done((bf16[32,128,128]{2,1,0:T(8,128)(2,1)}, bf16[32,128,128]{2,1,0:T(8,128)(2,1)}, u32[]{:S(2)}, u32[]{:S(2)}) %collective-permute-start.5) | collective-permute-done | bytes 1048608 | tf_op jit(solution)/shard_map/ppermute | solution.py:42
  102.6 3.3 %pad_maximum_fusion = bf16[96,128,128]{2,1,0:T(8,128)(2,1)} fusion(bf16[32,128,128]{2,1,0:T(8,128)(2,1)} %collective-permute-done.6, bf16[32,128,128]{2,1,0:T(8,128)(2,1)} %bitcast.6, bf16[32,128,128]{2,1,0:T(8,128)(2,1)} %collective-permute-done.5), kind=kLoop, calls=%fused_computation.9 | loop fusion | flops 3145728 | bytes 6291456 | tf_op jit(solution)/shard_map/concatenate | solution.py:40
  105.9 10.5 %gather_fusion = bf16[256,128,128]{2,1,0:T(8,128)(2,1)} fusion(bf16[96,128,128]{2,1,0:T(8,128)(2,1)} %pad_maximum_fusion, s32[1024]{0:T(1024)S(1)} %pad_clamp_fusion), kind=kCustom, calls=%fused_computation | custom fusion | bytes 16778240 | tf_op jit(solution)/shard_map/gather | solution.py:78
  116.4 7.0 %bitcast_select_fusion = bf16[64,512,128]{2,1,0:T(8,128)(2,1)S(1)} fusion(pred[64,512]{1,0:T(8,128)(4,1)S(1)} %bitcast.27, bf16[64,512,128]{2,1,0:T(8,128)(2,1)} %bitcast.23), kind=kLoop, calls=%fused_computation.1 | loop fusion | flops 4194304 | bytes 16809984 | tf_op jit(solution)/shard_map/jit(_where)/select_n | solution.py:79
  123.4 7.0 %convolution_convert_fusion.1 = bf16[64,128,128]{1,2,0:T(8,128)(2,1)} fusion(bf16[64,128,512]{2,1,0:T(8,128)(2,1)} %param.8, bf16[64,512,128]{2,1,0:T(8,128)(2,1)S(1)} %bitcast_select_fusion), kind=kOutput, calls=%fused_computation.10 | convolution fusion | flops 1074790400 | bytes 18874368 | tf_op jit(solution)/shard_map/uij,ujc->uic/dot_general | solution.py:81
  (3 shorter events, 0.0 us)
Async XLA Ops:
  0.0 14.2 %copy-start = (bf16[32,128,384]{2,1,0:T(8,128)(2,1)S(1)}, bf16[32,128,384]{2,1,0:T(8,128)(2,1)}, u32[]{:S(2)}) copy-start(bf16[32,128,384]{2,1,0:T(8,128)(2,1)} %param.7) | copy-start | bytes 9437188
  0.9 10.0 %collective-permute-start = (bf16[128,128]{1,0:T(8,128)(2,1)S(1)}, bf16[128,128]{1,0:T(8,128)(2,1)S(1)}, u32[]{:S(2)}, u32[]{:S(2)}) collective-permute-start(bf16[128,128]{1,0:T(8,128)(2,1)S(1)} %get-tuple-element.7), channel_id=1, source_target_pairs={{0,4},{4,8},{8,12},{12,16},{16,20},{20,24},{24,28},{28,32},{32,36}... | collective-permute-start | bytes 98312 | tf_op jit(solution)/shard_map/ppermute | solution.py:42
  4.9 7.6 %collective-permute-start.1 = (bf16[128,128]{1,0:T(8,128)(2,1)S(1)}, bf16[128,128]{1,0:T(8,128)(2,1)S(1)}, u32[]{:S(2)}, u32[]{:S(2)}) collective-permute-start(bf16[128,128]{1,0:T(8,128)(2,1)S(1)} %get-tuple-element.8), channel_id=1, source_target_pairs={{4,0},{8,4},{12,8},{16,12},{20,16},{24,20},{28,24},{32,28},{36,32}... | collective-permute-start | bytes 98312 | tf_op jit(solution)/shard_map/ppermute | solution.py:44
  17.4 25.6 %collective-permute-start.2 = (bf16[4096,128]{1,0:T(8,128)(2,1)}, bf16[4096,128]{1,0:T(8,128)(2,1)}, u32[]{:S(2)}, u32[]{:S(2)}) collective-permute-start(bf16[4096,128]{1,0:T(8,128)(2,1)} %bitcast.4), channel_id=1, source_target_pairs={{0,1},{1,2},{2,3},{3,0},{4,5},{5,6},{6,7},{7,4},{8,9},{9,10},{10,1... | collective-permute-start | bytes 3145736 | tf_op jit(solution)/shard_map/ppermute | solution.py:23
  18.9 27.6 %collective-permute-start.3 = (bf16[4096,128]{1,0:T(8,128)(2,1)}, bf16[4096,128]{1,0:T(8,128)(2,1)}, u32[]{:S(2)}, u32[]{:S(2)}) collective-permute-start(bf16[4096,128]{1,0:T(8,128)(2,1)} %bitcast.4), channel_id=1, source_target_pairs={{0,3},{1,0},{2,1},{3,2},{4,7},{5,4},{6,5},{7,6},{8,11},{9,8},{10,9... | collective-permute-start | bytes 3145736 | tf_op jit(solution)/shard_map/ppermute | solution.py:26
  43.0 24.5 %collective-permute-start.4 = (bf16[4096,128]{1,0:T(8,128)(2,1)}, bf16[4096,128]{1,0:T(8,128)(2,1)S(1)}, u32[]{:S(2)}, u32[]{:S(2)}) collective-permute-start(bf16[4096,128]{1,0:T(8,128)(2,1)} %collective-permute-done.2), channel_id=1, source_target_pairs={{0,1},{1,2},{2,3},{3,0},{4,5},{5,6},{6,7},{7,4},{8,9},{9,10},{10,1... | collective-permute-start | bytes 3145736 | tf_op jit(solution)/shard_map/ppermute | solution.py:23
  48.0 30.8 %copy-start.1 = (s32[64]{0:T(128)S(1)}, s32[64]{0:T(128)}, u32[]{:S(2)}) copy-start(s32[64]{0:T(128)} %param.11) | copy-start | bytes 772
  48.0 31.0 %copy-start.2 = (s32[64]{0:T(128)S(1)}, s32[64]{0:T(128)}, u32[]{:S(2)}) copy-start(s32[64]{0:T(128)} %param.10) | copy-start | bytes 772
  71.0 25.5 %collective-permute-start.6 = (bf16[32,128,128]{2,1,0:T(8,128)(2,1)}, bf16[32,128,128]{2,1,0:T(8,128)(2,1)}, u32[]{:S(2)}, u32[]{:S(2)}) collective-permute-start(bf16[32,128,128]{2,1,0:T(8,128)(2,1)} %bitcast.6), channel_id=1, source_target_pairs={{4,0},{8,4},{12,8},{16,12},{20,16},{24,20},{28,24},{32,28},{36,32}... | collective-permute-start | bytes 3145736 | tf_op jit(solution)/shard_map/ppermute | solution.py:44
  76.7 25.9 %collective-permute-start.5 = (bf16[32,128,128]{2,1,0:T(8,128)(2,1)}, bf16[32,128,128]{2,1,0:T(8,128)(2,1)}, u32[]{:S(2)}, u32[]{:S(2)}) collective-permute-start(bf16[32,128,128]{2,1,0:T(8,128)(2,1)} %bitcast.6), channel_id=1, source_target_pairs={{0,4},{4,8},{8,12},{12,16},{16,20},{20,24},{24,28},{28,32},{32,36}... | collective-permute-start | bytes 3145736 | tf_op jit(solution)/shard_map/ppermute | solution.py:42
